TPU v7x, 512 devices: a whole 4x8x8 slice. The times are simulated.
512 devices in a mesh: ctx: 32 (over z, y_hi), heads: 16 (over y_lo, x, core).
Axes of the slice: x: 4, y: 8 (y_hi: 4, y_lo: 2; y = y_hi * 2 + y_lo), z: 8, core: 2. Of those that a mesh axis runs over, the one named last changes fastest.
Arguments:
- resid_in: bfloat16 [4096, 5376], P('ctx', 'heads'), may hold values from -6 to 6
- first_layer_queries: bfloat16 [4096, 4096], P('ctx', 'heads'), may hold values from -270 to 270
- first_layer_keys: bfloat16 [4096, 2048], P('ctx', 'heads'), may hold values from -7 to 7
- first_layer_values: bfloat16 [4096, 2048], P('ctx', 'heads'), may hold values from -6 to 6
- out_one: bfloat16 [4096, 5376], P('heads'), may hold values from -6 to 6
- post_gain: float32 [5376], replicated, may hold values from 0.1 to 1.9
- pre_gain: float32 [5376], replicated, may hold values from 0.1 to 1.9
- proj_query: bfloat16 [5376, 4096], P('ctx', 'heads'), may hold values from -30 to 30
- key_projection: bfloat16 [5376, 2048], P('ctx', 'heads'), may hold values from -1 to 1
- value_projection: bfloat16 [5376, 2048], P('ctx', 'heads'), may hold values from -0.078125 to 0.078125
- window: int32 [32], P('heads'), may hold values from 512 to 1024, as said below
- positions: int32 [4096], replicated, may hold values from 0 to 2047, as said below
Outputs:
- resid_out: bfloat16 [4096, 5376], P('ctx', 'heads')
- attended: bfloat16 [4096, 4096], P('ctx', 'heads')
Inputs may be any that keep to these rules, and one draw needn't show every extreme that they name: Each query head's window counts back from and includes its own token; some head's window is exactly 1024. `positions`: tokens form three packed documents: a position is 0 at a document's first token and one more than the previous token's otherwise; one document has exactly 2048 tokens and none has more.
All inputs are finite; a program needn't handle non-finite values.
Results may differ from a plain program's by a relative error of at most 0.03.
Values may be sent and summed in bfloat16 or wider, within the bound.
No kernel may reach another device: no remote copies, remote signals or barrier semaphores. Data moves between devices by JAX's collectives and lax.ppermute only.
A program may use at most 64 MiB of HBM per device.

v0:
```python
from functools import partial
import jax
import jax.numpy as jnp
from jax import lax
from jax.sharding import PartitionSpec as P

HEAD_SIZE = 128
LONGEST_WINDOW = 1024
SCALE = 168.0 ** (-0.5)
EPS = 1e-06
THETA = 1000000.0
POSITION_FACTOR = 0.125


def shifted(value, axis, steps):
    count = lax.axis_size(axis)
    leading, last = (max(0, -steps), min(count, count - steps))
    return lax.ppermute(value, axis, [(source, source + steps) for source in range(leading, last)])


def from_partner(block, axis, bit):
    count = lax.axis_size(axis)
    route = []
    for low in range(count):
        high = low | 1 << bit
        if high != low and high < count:
            route += [(low, high), (high, low)]
    return lax.ppermute(block, axis, route)


def apply_rotary(values, pos_rows, factor):
    half_dim = values.shape[-1] // 2
    speeds = THETA ** (-(jnp.arange(half_dim, dtype=jnp.float32) * 2.0 / values.shape[-1]))
    angles = (pos_rows.astype(jnp.float32) * factor)[:, None] * speeds[None, :]
    cosine = jnp.cos(angles)[:, None, :]
    sine_part = jnp.sin(angles)[:, None, :]
    front_half = values[..., :half_dim]
    back_half = values[..., half_dim:]
    return jnp.concatenate(
        [front_half * cosine - back_half * sine_part, back_half * cosine + front_half * sine_part],
        axis=-1,
    )


def lookup(position_table, tokens):
    return jnp.take(position_table, jnp.clip(tokens, 0, position_table.shape[0] - 1))


def zig_token(row_ids, tok_dev):
    half_rows = tok_dev // 2
    device_of = row_ids // tok_dev
    local_row = row_ids % tok_dev
    last_pair = 2 * lax.axis_size("ctx") - 1
    return jnp.where(
        local_row < half_rows,
        2 * device_of * half_rows + local_row,
        (last_pair - 2 * device_of) * half_rows + local_row - half_rows,
    )


def masked_attention(
    query_row_block,
    key_row_block,
    value_row_block,
    query_tok,
    key_tok,
    query_pos,
    key_pos,
    window_limits,
):
    scores = (
        jnp.einsum(
            "qagd,kad->qagk", query_row_block, key_row_block, preferred_element_type=jnp.float32
        )
        * SCALE
    )
    distance = query_tok[:, None] - key_tok[None, :]
    base_ok = (
        (distance >= 0)
        & (key_tok[None, :] >= 0)
        & (query_pos[:, None] - key_pos[None, :] == distance)
    )
    visible = base_ok[:, None, None, :] & (
        distance[:, None, None, :] < window_limits[None, :, :, None]
    )
    row_peak = jnp.max(jnp.where(visible, scores, -1e30), axis=-1, keepdims=True)
    lifted = jnp.where(visible, jnp.exp(scores - row_peak), 0.0)
    row_total = jnp.sum(lifted, axis=-1)
    mixed = jnp.einsum(
        "qagk,kad->qagd",
        lifted.astype(jnp.bfloat16),
        value_row_block,
        preferred_element_type=jnp.float32,
    )
    return (mixed / row_total[..., None]).astype(jnp.bfloat16)


def mirror(rows_block, mover):
    half_rows = rows_block.shape[0] // 2
    travel = rows_block[half_rows:]
    bit_count = lax.axis_size("ctx").bit_length() - 1
    for bit_index in range(bit_count):
        travel = mover(travel, bit_index)
    return jnp.concatenate([rows_block[:half_rows], travel], axis=0)


def project(residual_rows, pre_gain, proj_query, key_projection, value_projection, row_pos):
    row_count = residual_rows.shape[0]
    widened = residual_rows.astype(jnp.float32)
    normalized_rows = (
        pre_gain[None, :]
        * widened
        * lax.rsqrt(jnp.mean(widened * widened, axis=1, keepdims=True) + EPS)
    ).astype(jnp.bfloat16)
    query_heads = proj_query.shape[1] // HEAD_SIZE
    pair_heads = key_projection.shape[1] // HEAD_SIZE
    second_layer_query = (
        apply_rotary(
            jnp.dot(
                normalized_rows,
                lax.all_gather(proj_query, "ctx", axis=0, tiled=True),
                preferred_element_type=jnp.float32,
            ).reshape(row_count, query_heads, HEAD_SIZE),
            row_pos,
            POSITION_FACTOR,
        )
        .astype(jnp.bfloat16)
        .reshape(row_count, query_heads * HEAD_SIZE)
    )
    second_layer_key = (
        apply_rotary(
            jnp.dot(
                normalized_rows,
                lax.all_gather(key_projection, "ctx", axis=0, tiled=True),
                preferred_element_type=jnp.float32,
            ).reshape(row_count, pair_heads, HEAD_SIZE),
            row_pos,
            POSITION_FACTOR,
        )
        .astype(jnp.bfloat16)
        .reshape(row_count, pair_heads * HEAD_SIZE)
    )
    second_layer_value = jnp.dot(
        normalized_rows,
        lax.all_gather(value_projection, "ctx", axis=0, tiled=True),
        preferred_element_type=jnp.float32,
    ).astype(jnp.bfloat16)
    return (second_layer_query, second_layer_key, second_layer_value)


def attend_block(
    state, query_row_block, key_block, value_block, query_tok, query_pos, block_tok, block_pos
):
    row_peak, row_total, weighted = state
    scores = (
        jnp.einsum("qagd,kad->qagk", query_row_block, key_block, preferred_element_type=jnp.float32)
        * SCALE
    )
    distance = query_tok[:, None] - block_tok[None, :]
    visible = (distance >= 0) & (query_pos[:, None] - block_pos[None, :] == distance)
    visible = visible[:, None, None, :]
    new_peak = jnp.maximum(row_peak, jnp.max(jnp.where(visible, scores, -1e30), axis=-1))
    lifted = jnp.where(visible, jnp.exp(scores - new_peak[..., None]), 0.0)
    shrink = jnp.exp(row_peak - new_peak)
    row_total = row_total * shrink + jnp.sum(lifted, axis=-1)
    weighted = weighted * shrink[..., None] + jnp.einsum(
        "qagk,kad->qagd",
        lifted.astype(jnp.bfloat16),
        value_block,
        preferred_element_type=jnp.float32,
    )
    return (new_peak, row_total, weighted)


def keep_state(state):
    return state


def shards(
    resid_in,
    first_layer_queries,
    first_layer_keys,
    first_layer_values,
    out_one,
    post_gain,
    pre_gain,
    proj_query,
    key_projection,
    value_projection,
    window,
    positions,
):
    tok_dev = resid_in.shape[0]
    col_width = resid_in.shape[1]
    ctx_place = lax.axis_index("ctx")
    head_place = lax.axis_index("heads")
    query_heads = first_layer_queries.shape[1] // HEAD_SIZE
    pair_heads = first_layer_keys.shape[1] // HEAD_SIZE
    group_length = query_heads // pair_heads
    window_limits = window.reshape(pair_heads, group_length)
    own_pairs = jnp.stack([first_layer_keys, first_layer_values])
    reach_count = LONGEST_WINDOW // tok_dev
    pieces = [own_pairs]
    for section in range(reach_count):
        pieces = [shifted(own_pairs, "ctx", section + 1)] + pieces
    extended = jnp.concatenate(pieces, axis=1)
    key_span = extended.shape[1]
    local_tok = ctx_place * tok_dev + jnp.arange(tok_dev, dtype=jnp.int32)
    key_tok = (ctx_place - reach_count) * tok_dev + jnp.arange(key_span, dtype=jnp.int32)
    attend_one = masked_attention(
        first_layer_queries.reshape(tok_dev, pair_heads, group_length, HEAD_SIZE),
        extended[0].reshape(key_span, pair_heads, HEAD_SIZE),
        extended[1].reshape(key_span, pair_heads, HEAD_SIZE),
        local_tok,
        key_tok,
        lookup(positions, local_tok),
        lookup(positions, key_tok),
        window_limits,
    )
    attend_one = attend_one.reshape(tok_dev, query_heads * HEAD_SIZE)
    partial_rows = jnp.dot(attend_one, out_one, preferred_element_type=jnp.float32)
    mirror_tok = zig_token(ctx_place * tok_dev + jnp.arange(tok_dev, dtype=jnp.int32), tok_dev)
    mirror_pos = lookup(positions, mirror_tok)
    summed = lax.psum(partial_rows.astype(jnp.bfloat16), "heads").astype(jnp.float32)
    post_scaled = summed * lax.rsqrt(jnp.mean(summed * summed, axis=1, keepdims=True) + EPS)
    resid_full = lax.all_gather(resid_in, "heads", axis=1, tiled=True)
    residual_rows = (resid_full.astype(jnp.float32) + post_gain[None, :] * post_scaled).astype(
        jnp.bfloat16
    )
    resid_out = lax.dynamic_slice_in_dim(residual_rows, head_place * col_width, col_width, 1)
    second_layer_query, second_layer_key, second_layer_value = project(
        residual_rows,
        pre_gain,
        proj_query,
        key_projection,
        value_projection,
        lookup(positions, local_tok),
    )
    merged = jnp.concatenate([second_layer_query, second_layer_key, second_layer_value], axis=1)

    def move_proj(piece, bit_index):
        return from_partner(piece, "ctx", bit_index)

    merged = mirror(merged, move_proj)
    query_cols = query_heads * HEAD_SIZE
    pair_cols = pair_heads * HEAD_SIZE
    second_layer_query = merged[:, :query_cols]
    second_layer_key = merged[:, query_cols : query_cols + pair_cols]
    second_layer_value = merged[:, query_cols + pair_cols :]
    half_rows = tok_dev // 2
    queries = second_layer_query.reshape(tok_dev, pair_heads, group_length, HEAD_SIZE)
    query_parts = (queries[:half_rows], queries[half_rows:])
    tok_parts = (mirror_tok[:half_rows], mirror_tok[half_rows:])
    pos_parts = (mirror_pos[:half_rows], mirror_pos[half_rows:])
    pair_two = jnp.stack([second_layer_key, second_layer_value])

    def empty_state():
        return (
            jnp.full((half_rows, pair_heads, group_length), -1e30, jnp.float32),
            jnp.zeros((half_rows, pair_heads, group_length), jnp.float32),
            jnp.zeros((half_rows, pair_heads, group_length, HEAD_SIZE), jnp.float32),
        )

    start_state = (empty_state(), empty_state())
    piece = lax.all_gather(pair_two, "ctx", axis=1, tiled=True)
    piece_rows = piece.shape[1]
    unit_rows = 2 * tok_dev
    unit_count = piece_rows // unit_rows

    def one_unit(index, state):
        offset = index * unit_rows
        unit_block = lax.dynamic_slice_in_dim(piece, offset, unit_rows, 1)
        current = list(state)
        for key_half in range(unit_rows // half_rows):
            key_block = unit_block[0, key_half * half_rows : (key_half + 1) * half_rows].reshape(
                half_rows, pair_heads, HEAD_SIZE
            )
            value_block = unit_block[1, key_half * half_rows : (key_half + 1) * half_rows].reshape(
                half_rows, pair_heads, HEAD_SIZE
            )
            key_row_block = offset + key_half * half_rows + jnp.arange(half_rows, dtype=jnp.int32)
            block_tok = zig_token(key_row_block, tok_dev)
            block_pos = lookup(positions, block_tok)
            earliest = jnp.min(block_tok)
            for query_half in range(2):
                work = partial(
                    attend_block,
                    query_row_block=query_parts[query_half],
                    key_block=key_block,
                    value_block=value_block,
                    query_tok=tok_parts[query_half],
                    query_pos=pos_parts[query_half],
                    block_tok=block_tok,
                    block_pos=block_pos,
                )
                needed = earliest <= tok_parts[query_half][half_rows - 1]
                current[query_half] = lax.cond(needed, work, keep_state, current[query_half])
        return tuple(current)

    final_state = lax.fori_loop(0, unit_count, one_unit, start_state)
    front = final_state[0][2] / final_state[0][1][..., None]
    back = final_state[1][2] / final_state[1][1][..., None]
    attended = (
        jnp.concatenate([front, back], axis=0)
        .astype(jnp.bfloat16)
        .reshape(tok_dev, query_heads * HEAD_SIZE)
    )
    return (resid_out, attended)


def solution(mesh):
    placed = (
        P("ctx", "heads"),
        P("ctx", "heads"),
        P("ctx", "heads"),
        P("ctx", "heads"),
        P("heads", None),
        P(),
        P(),
        P("ctx", "heads"),
        P("ctx", "heads"),
        P("ctx", "heads"),
        P("heads"),
        P(),
    )
    return jax.shard_map(
        shards,
        mesh=mesh,
        in_specs=placed,
        out_specs=(P("ctx", "heads"), P("ctx", "heads")),
        check_vma=False,
    )
```

profile of v0, /device:TPU:2, one launch (start us, length us, event | category | flops | bytes accessed | tf_op | source)
XLA Modules:
  0.0 968.1 jit_solution(9957120319989894820)
XLA Ops:
  8.2 6.1 collective-permute-start
  14.3 8.0 collective-permute-start.1
  22.2 7.7 collective-permute-start.2
  30.0 5.4 collective-permute-start.3
  35.4 3.4 collective-permute-start.4
  40.6 6.5 gather_fusion.4
  50.8 6.6 collective-permute-start.6
  67.2 123.5 %all-reduce.2.cloned.1.call-done = bf16[128,5376]{1,0:T(8,128)(2,1)} async-done(((bf16[128,5376]{1,0:T(8,128)(2,1)}), bf16[128,5376]{1,0:T(8,128)(2,1)}) %all-reduce.2.cloned.1.call-update) | async-done | bytes 1376272 | tf_op jit(solution)/shard_map/psum | solution.py:224
  192.4 41.8 %all-gather.6.cloned.1.call-done = bf16[128,5376]{0,1:T(8,128)(2,1)} async-done(((bf16[128,336]{0,1:T(8,128)(2,1)}), bf16[128,5376]{0,1:T(8,128)(2,1)}) %all-gather.6.cloned.1.call-update) | async-done | bytes 1376272 | tf_op jit(solution)/shard_map/all_gather | solution.py:226
  236.8 3.8 fusion.130
  240.6 81.4 %all-gather.10.cloned.1.call-done = bf16[5376,128]{1,0:T(8,128)(2,1)} async-done(((bf16[168,128]{1,0:T(8,128)(2,1)}), bf16[5376,128]{1,0:T(8,128)(2,1)}) %all-gather.10.cloned.1.call-update) | async-done | bytes 1376272 | tf_op jit(solution)/shard_map/all_gather | solution.py:134
  324.7 80.3 %all-gather.12.cloned.1.call-done = bf16[5376,128]{1,0:T(8,128)(2,1)} async-done(((bf16[168,128]{1,0:T(8,128)(2,1)}), bf16[5376,128]{1,0:T(8,128)(2,1)}) %all-gather.12.cloned.1.call-update) | async-done | bytes 1376272 | tf_op jit(solution)/shard_map/all_gather | solution.py:145
  407.6 86.1 %all-gather.8.cloned.1.call-done = bf16[5376,256]{1,0:T(8,128)(2,1)} async-done(((bf16[168,256]{1,0:T(8,128)(2,1)}), bf16[5376,256]{1,0:T(8,128)(2,1)}) %all-gather.8.cloned.1.call-update) | async-done | bytes 2752528 | tf_op jit(solution)/shard_map/all_gather | solution.py:121
  493.7 3.4 fusion.164
  497.3 4.5 collective-permute-start.8
  501.9 4.6 collective-permute-done.8
  506.5 4.3 collective-permute-start.9
  510.8 7.9 collective-permute-done.9
  521.3 5.4 collective-permute-done.10
  528.6 10.0 %collective-permute-done.11 = bf16[64,512]{0,1:T(8,128)(2,1)S(1)} collective-permute-done((bf16[64,512]{0,1:T(8,128)(2,1)S(1)}, bf16[64,512]{0,1:T(8,128)(2,1)S(1)}, u32[]{:S(2)}, u32[]{:S(2)}) %collective-permute-start.11) | collective-permute-done | bytes 65568 | tf_op jit(solution)/shard_map/ppermute | solution.py:28
  538.6 4.0 collective-permute-start.12
  542.6 7.1 collective-permute-done.12
  553.8 75.9 %all-gather.14.cloned.1.call-done = bf16[2,4096,128]{1,2,0:T(8,128)(2,1)} async-done(((bf16[2,128,128]{1,2,0:T(8,128)(2,1)}), bf16[2,4096,128]{1,2,0:T(8,128)(2,1)}) %all-gather.14.cloned.1.call-update) | async-done | bytes 2097168 | tf_op jit(solution)/shard_map/all_gather | solution.py:265
  629.8 330.5 %while.26 = (s32[]{:T(128)}, f32[64,1,2]{0,2,1:T(2,128)S(1)}, f32[64,1,2]{0,2,1:T(2,128)S(1)}, f32[64,1,2,128]{3,0,2,1:T(8,128)S(1)}, f32[64,1,2]{0,2,1:T(2,128)...) while((s32[]{:T(128)}, f32[64,1,2]{0,2,1:T(2,128)S(1)}, ...), condition=%wide.region_42.45_spmd, body=%wide.region_5.44_spmd.sunk | while | flops 34610448 | bytes 3114491 | solution.py:300
  (1152 shorter events, 231.8 us)
Async XLA Ops:
  7.2 55.4 %copy-start = (bf16[256,5376]{1,0:T(8,128)(2,1)S(1)}, bf16[256,5376]{1,0:T(8,128)(2,1)}, u32[]{:S(2)}) copy-start(bf16[256,5376]{1,0:T(8,128)(2,1)} %param.38) | copy-start | bytes 8257540
  7.2 33.4 %copy-start.1 = (s32[4096]{0:T(1024)S(1)}, s32[4096]{0:T(1024)}, u32[]{:S(2)}) copy-start(s32[4096]{0:T(1024)} %param.45) | copy-start | bytes 49156
  7.2 183.5 %all-reduce.2.cloned.1.call-start = ((), (), s32[]{:S(2)}) async-start(), calls=%async_computation.1 | async-start | bytes 2752512 | tf_op jit(solution)/shard_map/psum | solution.py:224
  8.2 40.3 %collective-permute-start = (bf16[2,128,128]{2,1,0:T(8,128)(2,1)S(1)}, bf16[2,128,128]{2,1,0:T(8,128)(2,1)S(1)}, u32[]{:S(2)}, u32[]{:S(2)}) collective-permute-start(bf16[2,128,128]{2,1,0:T(8,128)(2,1)S(1)} %pad_maximum_fusion.2), channel_id=1, source_target_pairs={{0,128},{16,144},{32,160},{48,176},{64,192},{80,208},{96,224},{112... | collective-permute-start | bytes 196616 | tf_op jit(solution)/shard_map/ppermute | solution.py:18
  14.3 36.5 %collective-permute-start.1 = (bf16[2,128,128]{2,1,0:T(8,128)(2,1)S(1)}, bf16[2,128,128]{2,1,0:T(8,128)(2,1)S(1)}, u32[]{:S(2)}, u32[]{:S(2)}) collective-permute-start(bf16[2,128,128]{2,1,0:T(8,128)(2,1)S(1)} %pad_maximum_fusion.2), channel_id=1, source_target_pairs={{0,112},{16,128},{32,144},{48,160},{64,176},{80,192},{96,208},{112... | collective-permute-start | bytes 196616 | tf_op jit(solution)/shard_map/ppermute | solution.py:18
  22.2 35.1 %collective-permute-start.2 = (bf16[2,128,128]{2,1,0:T(8,128)(2,1)S(1)}, bf16[2,128,128]{2,1,0:T(8,128)(2,1)S(1)}, u32[]{:S(2)}, u32[]{:S(2)}) collective-permute-start(bf16[2,128,128]{2,1,0:T(8,128)(2,1)S(1)} %pad_maximum_fusion.2), channel_id=1, source_target_pairs={{0,96},{16,112},{32,128},{48,144},{64,160},{80,176},{96,192},{112,... | collective-permute-start | bytes 196616 | tf_op jit(solution)/shard_map/ppermute | solution.py:18
  30.0 28.7 %collective-permute-start.3 = (bf16[2,128,128]{2,1,0:T(8,128)(2,1)S(1)}, bf16[2,128,128]{2,1,0:T(8,128)(2,1)S(1)}, u32[]{:S(2)}, u32[]{:S(2)}) collective-permute-start(bf16[2,128,128]{2,1,0:T(8,128)(2,1)S(1)} %pad_maximum_fusion.2), channel_id=1, source_target_pairs={{0,80},{16,96},{32,112},{48,128},{64,144},{80,160},{96,176},{112,1... | collective-permute-start | bytes 196616 | tf_op jit(solution)/shard_map/ppermute | solution.py:18
  35.4 23.3 %collective-permute-start.4 = (bf16[2,128,128]{2,1,0:T(8,128)(2,1)S(1)}, bf16[2,128,128]{2,1,0:T(8,128)(2,1)S(1)}, u32[]{:S(2)}, u32[]{:S(2)}) collective-permute-start(bf16[2,128,128]{2,1,0:T(8,128)(2,1)S(1)} %pad_maximum_fusion.2), channel_id=1, source_target_pairs={{0,64},{16,80},{32,96},{48,112},{64,128},{80,144},{96,160},{112,17... | collective-permute-start | bytes 196616 | tf_op jit(solution)/shard_map/ppermute | solution.py:18
  47.1 14.0 %copy-start.5 = (s32[2]{0:T(128)S(1)}, s32[2]{0:T(128)}, u32[]{:S(2)}) copy-start(s32[2]{0:T(128)} %param.44) | copy-start | bytes 28
  48.5 10.3 %collective-permute-start.5 = (bf16[2,128,128]{2,1,0:T(8,128)(2,1)S(1)}, bf16[2,128,128]{2,1,0:T(8,128)(2,1)S(1)}, u32[]{:S(2)}, u32[]{:S(2)}) collective-permute-start(bf16[2,128,128]{2,1,0:T(8,128)(2,1)S(1)} %pad_maximum_fusion.2), channel_id=1, source_target_pairs={{0,48},{16,64},{32,80},{48,96},{64,112},{80,128},{96,144},{112,160... | collective-permute-start | bytes 196616 | tf_op jit(solution)/shard_map/ppermute | solution.py:18
  50.8 8.5 collective-permute-start.6
  57.4 3.7 collective-permute-start.7
  64.3 169.9 %all-gather.6.cloned.1.call-start = ((), (), s32[]{:S(2)}) async-start(), calls=%async_computation | async-start | bytes 1462272 | tf_op jit(solution)/shard_map/all_gather | solution.py:226
  65.1 256.9 %all-gather.10.cloned.1.call-start = ((), (), s32[]{:S(2)}) async-start(), calls=%async_computation.3 | async-start | bytes 1419264 | tf_op jit(solution)/shard_map/all_gather | solution.py:134
  65.8 339.2 %all-gather.12.cloned.1.call-start = ((), (), s32[]{:S(2)}) async-start(), calls=%async_computation.4 | async-start | bytes 1419264 | tf_op jit(solution)/shard_map/all_gather | solution.py:145
  66.4 427.3 %all-gather.8.cloned.1.call-start = ((), (), s32[]{:S(2)}) async-start(), calls=%async_computation.2 | async-start | bytes 2838528 | tf_op jit(solution)/shard_map/all_gather | solution.py:121
  67.0 562.7 %all-gather.14.cloned.1.call-start = ((), (), s32[]{:S(2)}) async-start(), calls=%async_computation.5 | async-start | bytes 2162688 | tf_op jit(solution)/shard_map/all_gather | solution.py:265
  192.4 44.4 %copy-start.4 = (f32[5376]{0:T(1024)S(1)}, f32[5376]{0:T(1024)}, u32[]{:S(2)}) copy-start(f32[5376]{0:T(1024)} %param.39) | copy-start | bytes 64516
  236.8 85.2 %copy-start.7 = (f32[5376]{0:T(1024)S(1)}, f32[5376]{0:T(1024)}, u32[]{:S(2)}) copy-start(f32[5376]{0:T(1024)} %param.40) | copy-start | bytes 64516
  497.3 9.2 collective-permute-start.8
  506.5 12.2 %collective-permute-start.9 = (bf16[64,512]{0,1:T(8,128)(2,1)S(1)}, bf16[64,512]{0,1:T(8,128)(2,1)S(1)}, u32[]{:S(2)}, u32[]{:S(2)}) collective-permute-start(bf16[64,512]{0,1:T(8,128)(2,1)S(1)} %collective-permute-done.8), channel_id=1, source_target_pairs={{0,32},{32,0},{16,48},{48,16},{64,96},{96,64},{80,112},{112,80},{1... | collective-permute-start | bytes 196616 | tf_op jit(solution)/shard_map/ppermute | solution.py:28
  518.7 8.0 collective-permute-start.10
  526.6 12.0 %collective-permute-start.11 = (bf16[64,512]{0,1:T(8,128)(2,1)S(1)}, bf16[64,512]{0,1:T(8,128)(2,1)S(1)}, u32[]{:S(2)}, u32[]{:S(2)}) collective-permute-start(bf16[64,512]{0,1:T(8,128)(2,1)S(1)} %collective-permute-done.10), channel_id=1, source_target_pairs={{0,128},{128,0},{16,144},{144,16},{32,160},{160,32},{48,176},{176,... | collective-permute-start | bytes 196616 | tf_op jit(solution)/shard_map/ppermute | solution.py:28
  538.6 11.1 %collective-permute-start.12 = (bf16[64,512]{0,1:T(8,128)(2,1)S(1)}, bf16[64,512]{0,1:T(8,128)(2,1)S(1)}, u32[]{:S(2)}, u32[]{:S(2)}) collective-permute-start(bf16[64,512]{0,1:T(8,128)(2,1)S(1)} %collective-permute-done.11), channel_id=1, source_target_pairs={{0,256},{256,0},{16,272},{272,16},{32,288},{288,32},{48,304},{304,... | collective-permute-start | bytes 196616 | tf_op jit(solution)/shard_map/ppermute | solution.py:28
  (3 other events, 42.0 us)
Sparse Core Ops, SparseCore 0:
  64.5 126.2 all-reduce.1
  192.9 41.3 all-gather.5
  237.5 84.5 all-gather.9
  325.1 79.9 all-gather.11
  408.1 85.5 all-gather.7
  550.6 79.0 all-gather.13
where the time goes:
time: 972 us; the launch traced here: 968 us
  waiting for transfers between devices  529 us (54%)
  loops' own time  173 us (18%)
  local copies, waits for them, and re-layouts  113 us (12%)
  starting transfers between devices  58.4 us (6%)
  other arithmetic  44 us (5%)
  matrix products  36.2 us (4%)
  between operations  14.7 us (2%)
    another operation x1, loops' own time, shards(): final_state = lax.fori_loop(0, unit_count, one_unit, start_state)  169 us
    psum x1, waiting for transfers between devices, shards(): lax.psum(partial_rows.astype(jnp.bfloat16), 'heads').astype(jnp.float32)  123 us
    all_gather x1, waiting for transfers between devices, project(): lax.all_gather(proj_query, 'ctx', axis=0, tiled=True)  86.1 us
    all_gather x1, waiting for transfers between devices, project(): lax.all_gather(key_projection, 'ctx', axis=0, tiled=True)  81.4 us
    all_gather x1, waiting for transfers between devices, project(): lax.all_gather(value_projection, 'ctx', axis=0, tiled=True)  80.3 us
    all_gather x1, waiting for transfers between devices, shards(): piece = lax.all_gather(pair_two, 'ctx', axis=1, tiled=True)  75.9 us
    gather x67, local copies, waits for them, and re-layouts, lookup(): jnp.take(position_table, jnp.clip(tokens, 0, position_table.shape[0] - 1))  58.9 us
    all_gather x1, waiting for transfers between devices, shards(): resid_full = lax.all_gather(resid_in, 'heads', axis=1, tiled=True)  41.8 us
  transfers between devices with their start and end apart: 19, of which 13 were waited for; matrix products, arithmetic and copies ran while one was open for 3% of the time, Pallas kernels for 0%

commit v1 on v0

--- a/solution.py
+++ b/solution.py
@@ -221,7 +221,9 @@
     partial_rows = jnp.dot(attend_one, out_one, preferred_element_type=jnp.float32)
     mirror_tok = zig_token(ctx_place * tok_dev + jnp.arange(tok_dev, dtype=jnp.int32), tok_dev)
     mirror_pos = lookup(positions, mirror_tok)
-    summed = lax.psum(partial_rows.astype(jnp.bfloat16), "heads").astype(jnp.float32)
+    summed = jnp.sum(lax.all_gather(partial_rows.astype(jnp.bfloat16), "heads"), axis=0).astype(
+        jnp.float32
+    )
     post_scaled = summed * lax.rsqrt(jnp.mean(summed * summed, axis=1, keepdims=True) + EPS)
     resid_full = lax.all_gather(resid_in, "heads", axis=1, tiled=True)
     residual_rows = (resid_full.astype(jnp.float32) + post_gain[None, :] * post_scaled).astype(

time: 972 us -> 926 us (0.953)
  waiting for transfers between devices: 529 us -> 479 us
  other arithmetic: 44 us -> 58.2 us
    psum x1 -> x0, waiting for transfers between devices: 123 us -> none  [shards(): lax.psum(partial_rows.astype(jnp.bfloat16), 'heads').astype(jnp.float32)]
    all_gather x0 -> x1, waiting for transfers between devices: none -> 121 us  [shards(): lax.all_gather(partial_rows.astype(jnp.bfloat16), 'heads')]
    all_gather x1, waiting for transfers between devices: 41.8 us -> 3.76 us  [shards(): resid_full = lax.all_gather(resid_in, 'heads', axis=1, tiled=True)]
    reduce_sum x0 -> x1, other arithmetic: none -> 13.3 us  [shards(): jnp.sum(lax.all_gather(partial_rows.astype(jnp.bfloat16), 'heads'), axis=0)]
    all_gather x1, waiting for transfers between devices: 86.1 us -> 75.6 us  [project(): lax.all_gather(proj_query, 'ctx', axis=0, tiled=True)]
  transfers between devices with their start and end apart: 19 -> 19, of which waited for: 13 -> 13; matrix products, arithmetic and copies ran while one was open for 3% -> 5% of each run, Pallas kernels for 0% -> 0%
where the time goes in v1:
time: 926 us; the launch traced here: 922 us
  waiting for transfers between devices  479 us (52%)
  loops' own time  164 us (18%)
  local copies, waits for them, and re-layouts  111 us (12%)
  starting transfers between devices  58.4 us (6%)
  other arithmetic  58.2 us (6%)
  matrix products  36.3 us (4%)
  between operations  14.7 us (2%)
    another operation x1, loops' own time, shards(): final_state = lax.fori_loop(0, unit_count, one_unit, start_state)  160 us
    all_gather x1, waiting for transfers between devices, shards(): lax.all_gather(partial_rows.astype(jnp.bfloat16), 'heads')  121 us
    all_gather x1, waiting for transfers between devices, project(): lax.all_gather(key_projection, 'ctx', axis=0, tiled=True)  80.6 us
    all_gather x1, waiting for transfers between devices, project(): lax.all_gather(value_projection, 'ctx', axis=0, tiled=True)  80.3 us
    all_gather x1, waiting for transfers between devices, shards(): piece = lax.all_gather(pair_two, 'ctx', axis=1, tiled=True)  79.6 us
    all_gather x1, waiting for transfers between devices, project(): lax.all_gather(proj_query, 'ctx', axis=0, tiled=True)  75.6 us
    gather x67, local copies, waits for them, and re-layouts, lookup(): jnp.take(position_table, jnp.clip(tokens, 0, position_table.shape[0] - 1))  58.9 us
    ppermute x8, starting transfers between devices, shifted(): lax.ppermute(value, axis, [(source, source + steps) for source in range(l...  40.7 us
  transfers between devices with their start and end apart: 19, of which 13 were waited for; matrix products, arithmetic and copies ran while one was open for 5% of the time, Pallas kernels for 0%

profile of v1, /device:TPU:2, one launch (start us, length us, event | category | flops | bytes accessed | tf_op | source)
XLA Modules:
  0.0 921.9 jit_solution(10366004065899394700)
XLA Ops:
  8.2 6.1 collective-permute-start
  14.3 8.0 collective-permute-start.1
  22.2 7.7 collective-permute-start.2
  30.0 5.4 collective-permute-start.3
  35.4 3.4 collective-permute-start.4
  40.6 6.5 gather_fusion.4
  50.8 6.6 collective-permute-start.6
  66.6 3.8 all-gather.8.cloned.1.call-done
  72.9 121.4 %all-gather.18.cloned.1.call-done = bf16[2048,5376]{1,0:T(8,128)(2,1)} async-done(((bf16[128,5376]{1,0:T(8,128)(2,1)}), bf16[2048,5376]{1,0:T(8,128)(2,1)}) %all-gather.18.cloned.1.call-update) | async-done | bytes 22020112 | tf_op jit(solution)/shard_map/all_gather | solution.py:224
  194.3 13.3 %reduce_sum.128 = bf16[128,5376]{1,0:T(8,128)(2,1)} reduce(bf16[16,128,5376]{2,1,0:T(8,128)(2,1)} %bitcast.407, bf16[]{:T(256)} %constant.435.clone.1), dimensions={0}, to_apply=%region_2.4 | reduce | flops 10321920 | bytes 23396354 | tf_op jit(solution)/shard_map/reduce_sum | solution.py:224
  212.7 75.6 %all-gather.10.cloned.1.call-done = bf16[5376,256]{1,0:T(8,128)(2,1)} async-done(((bf16[168,256]{1,0:T(8,128)(2,1)}), bf16[5376,256]{1,0:T(8,128)(2,1)}) %all-gather.10.cloned.1.call-update) | async-done | bytes 2752528 | tf_op jit(solution)/shard_map/all_gather | solution.py:121
  288.4 3.4 fusion.164
  291.8 80.6 %all-gather.12.cloned.1.call-done = bf16[5376,128]{1,0:T(8,128)(2,1)} async-done(((bf16[168,128]{1,0:T(8,128)(2,1)}), bf16[5376,128]{1,0:T(8,128)(2,1)}) %all-gather.12.cloned.1.call-update) | async-done | bytes 1376272 | tf_op jit(solution)/shard_map/all_gather | solution.py:134
  375.2 80.3 %all-gather.14.cloned.1.call-done = bf16[5376,128]{1,0:T(8,128)(2,1)} async-done(((bf16[168,128]{1,0:T(8,128)(2,1)}), bf16[5376,128]{1,0:T(8,128)(2,1)}) %all-gather.14.cloned.1.call-update) | async-done | bytes 1376272 | tf_op jit(solution)/shard_map/all_gather | solution.py:145
  458.1 4.4 collective-permute-start.8
  462.5 4.8 collective-permute-done.8
  467.3 4.7 collective-permute-start.9
  472.0 7.3 collective-permute-done.9
  481.9 5.4 collective-permute-done.10
  489.2 9.0 collective-permute-done.11
  498.3 3.9 collective-permute-start.12
  502.2 7.3 collective-permute-done.12
  513.6 79.6 %all-gather.16.cloned.1.call-done = bf16[2,4096,128]{1,2,0:T(8,128)(2,1)} async-done(((bf16[2,128,128]{1,2,0:T(8,128)(2,1)}), bf16[2,4096,128]{1,2,0:T(8,128)(2,1)}) %all-gather.16.cloned.1.call-update) | async-done | bytes 2097168 | tf_op jit(solution)/shard_map/all_gather | solution.py:267
  593.3 320.9 %while.26 = (s32[]{:T(128)}, f32[64,1,2]{0,2,1:T(2,128)S(1)}, f32[64,1,2]{0,2,1:T(2,128)S(1)}, f32[64,1,2,128]{3,0,2,1:T(8,128)S(1)}, f32[64,1,2]{0,2,1:T(2,128)...) while((s32[]{:T(128)}, f32[64,1,2]{0,2,1:T(2,128)S(1)}, ...), condition=%wide.region_42.45_spmd, body=%wide.region_5.44_spmd.sunk | while | flops 34610448 | bytes 3114491 | solution.py:302
  (1155 shorter events, 233.4 us)
Async XLA Ops:
  7.2 55.5 %copy-start = (bf16[256,5376]{1,0:T(8,128)(2,1)S(1)}, bf16[256,5376]{1,0:T(8,128)(2,1)}, u32[]{:S(2)}) copy-start(bf16[256,5376]{1,0:T(8,128)(2,1)} %param.38) | copy-start | bytes 8257540
  7.2 33.5 %copy-start.1 = (s32[4096]{0:T(1024)S(1)}, s32[4096]{0:T(1024)}, u32[]{:S(2)}) copy-start(s32[4096]{0:T(1024)} %param.45) | copy-start | bytes 49156
  7.2 63.1 %all-gather.8.cloned.1.call-start = ((), (), s32[]{:S(2)}) async-start(), calls=%async_computation | async-start | bytes 1462272 | tf_op jit(solution)/shard_map/all_gather | solution.py:228
  8.2 40.4 %collective-permute-start = (bf16[2,128,128]{2,1,0:T(8,128)(2,1)S(1)}, bf16[2,128,128]{2,1,0:T(8,128)(2,1)S(1)}, u32[]{:S(2)}, u32[]{:S(2)}) collective-permute-start(bf16[2,128,128]{2,1,0:T(8,128)(2,1)S(1)} %pad_maximum_fusion.2), channel_id=1, source_target_pairs={{0,128},{16,144},{32,160},{48,176},{64,192},{80,208},{96,224},{112... | collective-permute-start | bytes 196616 | tf_op jit(solution)/shard_map/ppermute | solution.py:18
  14.3 36.6 %collective-permute-start.1 = (bf16[2,128,128]{2,1,0:T(8,128)(2,1)S(1)}, bf16[2,128,128]{2,1,0:T(8,128)(2,1)S(1)}, u32[]{:S(2)}, u32[]{:S(2)}) collective-permute-start(bf16[2,128,128]{2,1,0:T(8,128)(2,1)S(1)} %pad_maximum_fusion.2), channel_id=1, source_target_pairs={{0,112},{16,128},{32,144},{48,160},{64,176},{80,192},{96,208},{112... | collective-permute-start | bytes 196616 | tf_op jit(solution)/shard_map/ppermute | solution.py:18
  22.2 35.2 %collective-permute-start.2 = (bf16[2,128,128]{2,1,0:T(8,128)(2,1)S(1)}, bf16[2,128,128]{2,1,0:T(8,128)(2,1)S(1)}, u32[]{:S(2)}, u32[]{:S(2)}) collective-permute-start(bf16[2,128,128]{2,1,0:T(8,128)(2,1)S(1)} %pad_maximum_fusion.2), channel_id=1, source_target_pairs={{0,96},{16,112},{32,128},{48,144},{64,160},{80,176},{96,192},{112,... | collective-permute-start | bytes 196616 | tf_op jit(solution)/shard_map/ppermute | solution.py:18
  30.0 28.8 %collective-permute-start.3 = (bf16[2,128,128]{2,1,0:T(8,128)(2,1)S(1)}, bf16[2,128,128]{2,1,0:T(8,128)(2,1)S(1)}, u32[]{:S(2)}, u32[]{:S(2)}) collective-permute-start(bf16[2,128,128]{2,1,0:T(8,128)(2,1)S(1)} %pad_maximum_fusion.2), channel_id=1, source_target_pairs={{0,80},{16,96},{32,112},{48,128},{64,144},{80,160},{96,176},{112,1... | collective-permute-start | bytes 196616 | tf_op jit(solution)/shard_map/ppermute | solution.py:18
  35.4 23.4 %collective-permute-start.4 = (bf16[2,128,128]{2,1,0:T(8,128)(2,1)S(1)}, bf16[2,128,128]{2,1,0:T(8,128)(2,1)S(1)}, u32[]{:S(2)}, u32[]{:S(2)}) collective-permute-start(bf16[2,128,128]{2,1,0:T(8,128)(2,1)S(1)} %pad_maximum_fusion.2), channel_id=1, source_target_pairs={{0,64},{16,80},{32,96},{48,112},{64,128},{80,144},{96,160},{112,17... | collective-permute-start | bytes 196616 | tf_op jit(solution)/shard_map/ppermute | solution.py:18
  38.8 155.5 %all-gather.18.cloned.1.call-start = ((), (), s32[]{:S(2)}) async-start(), calls=%async_computation.5 | async-start | bytes 23396352 | tf_op jit(solution)/shard_map/all_gather | solution.py:224
  47.2 14.0 %copy-start.6 = (s32[2]{0:T(128)S(1)}, s32[2]{0:T(128)}, u32[]{:S(2)}) copy-start(s32[2]{0:T(128)} %param.44) | copy-start | bytes 28
  48.5 10.3 %collective-permute-start.5 = (bf16[2,128,128]{2,1,0:T(8,128)(2,1)S(1)}, bf16[2,128,128]{2,1,0:T(8,128)(2,1)S(1)}, u32[]{:S(2)}, u32[]{:S(2)}) collective-permute-start(bf16[2,128,128]{2,1,0:T(8,128)(2,1)S(1)} %pad_maximum_fusion.2), channel_id=1, source_target_pairs={{0,48},{16,64},{32,80},{48,96},{64,112},{80,128},{96,144},{112,160... | collective-permute-start | bytes 196616 | tf_op jit(solution)/shard_map/ppermute | solution.py:18
  50.8 8.5 collective-permute-start.6
  57.4 3.7 collective-permute-start.7
  64.4 224.0 %all-gather.10.cloned.1.call-start = ((), (), s32[]{:S(2)}) async-start(), calls=%async_computation.1 | async-start | bytes 2838528 | tf_op jit(solution)/shard_map/all_gather | solution.py:121
  65.1 307.3 %all-gather.12.cloned.1.call-start = ((), (), s32[]{:S(2)}) async-start(), calls=%async_computation.2 | async-start | bytes 1419264 | tf_op jit(solution)/shard_map/all_gather | solution.py:134
  65.7 389.8 %all-gather.14.cloned.1.call-start = ((), (), s32[]{:S(2)}) async-start(), calls=%async_computation.3 | async-start | bytes 1419264 | tf_op jit(solution)/shard_map/all_gather | solution.py:145
  66.3 526.9 %all-gather.16.cloned.1.call-start = ((), (), s32[]{:S(2)}) async-start(), calls=%async_computation.4 | async-start | bytes 2162688 | tf_op jit(solution)/shard_map/all_gather | solution.py:267
  194.3 15.1 %copy-start.5 = (f32[5376]{0:T(1024)S(1)}, f32[5376]{0:T(1024)}, u32[]{:S(2)}) copy-start(f32[5376]{0:T(1024)} %param.39) | copy-start | bytes 64516
  209.4 78.9 %copy-start.8 = (f32[5376]{0:T(1024)S(1)}, f32[5376]{0:T(1024)}, u32[]{:S(2)}) copy-start(f32[5376]{0:T(1024)} %param.40) | copy-start | bytes 64516
  458.1 9.2 collective-permute-start.8
  467.3 12.0 %collective-permute-start.9 = (bf16[64,512]{0,1:T(8,128)(2,1)S(1)}, bf16[64,512]{0,1:T(8,128)(2,1)S(1)}, u32[]{:S(2)}, u32[]{:S(2)}) collective-permute-start(bf16[64,512]{0,1:T(8,128)(2,1)S(1)} %collective-permute-done.8), channel_id=1, source_target_pairs={{0,32},{32,0},{16,48},{48,16},{64,96},{96,64},{80,112},{112,80},{1... | collective-permute-start | bytes 196616 | tf_op jit(solution)/shard_map/ppermute | solution.py:28
  479.3 8.1 collective-permute-start.10
  487.3 11.0 %collective-permute-start.11 = (bf16[64,512]{0,1:T(8,128)(2,1)S(1)}, bf16[64,512]{0,1:T(8,128)(2,1)S(1)}, u32[]{:S(2)}, u32[]{:S(2)}) collective-permute-start(bf16[64,512]{0,1:T(8,128)(2,1)S(1)} %collective-permute-done.10), channel_id=1, source_target_pairs={{0,128},{128,0},{16,144},{144,16},{32,160},{160,32},{48,176},{176,... | collective-permute-start | bytes 196616 | tf_op jit(solution)/shard_map/ppermute | solution.py:28
  498.3 11.2 %collective-permute-start.12 = (bf16[64,512]{0,1:T(8,128)(2,1)S(1)}, bf16[64,512]{0,1:T(8,128)(2,1)S(1)}, u32[]{:S(2)}, u32[]{:S(2)}) collective-permute-start(bf16[64,512]{0,1:T(8,128)(2,1)S(1)} %collective-permute-done.11), channel_id=1, source_target_pairs={{0,256},{256,0},{16,272},{272,16},{32,288},{288,32},{48,304},{304,... | collective-permute-start | bytes 196616 | tf_op jit(solution)/shard_map/ppermute | solution.py:28
  (4 other events, 43.9 us)
Sparse Core Ops, SparseCore 0:
  38.9 31.3 all-gather.7
  72.5 121.8 all-gather.17
  197.5 90.8 all-gather.9
  291.4 81.0 all-gather.11
  375.5 79.9 all-gather.13
  510.4 82.7 all-gather.15
